TPU v7x, 256 devices: a whole 4x4x8 slice. The times are simulated.
256 devices in a mesh: seq: 64 (over x, z, core), head: 4 (over y).
Axes of the slice: x: 4, y: 4, z: 8, core: 2. Of those that a mesh axis runs over, the one named last changes fastest.
Arguments:
- queries: bfloat16 [16384, 64, 128], P(('seq', 'head')), may hold values from -64 to 64
- key_vectors: bfloat16 [16384, 64, 128], P(('seq', 'head')), may hold values from -5 to 5
- value_vectors: bfloat16 [16384, 64, 128], P(('seq', 'head')), may hold values from -6 to 6
- key_blocks: int32 [128, 12], P('seq'), may hold values from -1 to 125, as said below
Outputs:
- attended: bfloat16 [16384, 64, 128], P(('seq', 'head'))
Inputs may be any that keep to these rules, and one draw needn't show every extreme that they name: `key_blocks`: entries 2j and 2j+1 of row b are -1 or distinct blocks c with c // 2 == b // 2 - 2**j, never b - 1.
All inputs are finite; a program needn't handle non-finite values.
Results may differ from a plain program's by a relative error of at most 0.004.
Values may be sent and summed in bfloat16 or wider, within the bound.
A program may use at most 192 MiB of HBM per device.

v0:
```python
import math
import jax
import jax.numpy as jnp
from jax import lax
from jax.sharding import PartitionSpec as P

BLOCK = 128
LEVELS = 6


def from_behind(value, axis, by):
    size = lax.axis_size(axis)
    pairs = [(i, i + by) for i in range(size) if 0 <= i + by < size]
    return lax.ppermute(value, axis, pairs)


def absorb(carried, scores, apply_values):
    running_max, running_sum, weighted = carried
    new_max = jnp.maximum(running_max, jnp.max(scores, axis=-1))
    factor = jnp.exp(running_max - new_max)
    weights = jnp.exp(scores - new_max[..., None])
    running_sum = running_sum * factor + jnp.sum(weights, axis=-1)
    weighted = weighted * jnp.transpose(factor, (0, 2, 1))[..., None] + apply_values(
        weights.astype(jnp.bfloat16)
    )
    return (new_max, running_sum, weighted)


def local(queries, key_vectors, value_vectors, key_blocks):
    query_local, key_local, value_local = (
        lax.all_to_all(queries, "head", split_axis=1, concat_axis=0, tiled=True),
        lax.all_to_all(key_vectors, "head", split_axis=1, concat_axis=0, tiled=True),
        lax.all_to_all(value_vectors, "head", split_axis=1, concat_axis=0, tiled=True),
    )
    local_rows, head_count, head_width = query_local.shape
    blocks = local_rows // BLOCK
    device = lax.axis_index("seq")
    inverse_root = 1.0 / math.sqrt(head_width)
    query_tiles = query_local.reshape(blocks, BLOCK, head_count, head_width)
    query_ids = device * blocks + jnp.arange(blocks, dtype=jnp.int32)
    causal = jnp.arange(BLOCK)[:, None] >= jnp.arange(BLOCK)[None, :]
    carried = (
        jnp.full((blocks, head_count, BLOCK), -1e30, jnp.float32),
        jnp.zeros((blocks, head_count, BLOCK), jnp.float32),
        jnp.zeros((blocks, BLOCK, head_count, head_width), jnp.float32),
    )

    def dense_set(carried, near_keys, near_values, key_ids, with_diagonal):
        key_count = key_ids.shape[0]
        scores = (
            jnp.einsum("bqhd,nhd->bhqn", query_tiles, near_keys, preferred_element_type=jnp.float32)
            * inverse_root
        )
        scores = scores.reshape(blocks, head_count, BLOCK, key_count, BLOCK)
        listed = jnp.any(key_blocks[:, :, None] == key_ids[None, None, :], axis=1)
        window = key_ids[None, :] == query_ids[:, None] - 1
        allowed = (listed | window) & (key_ids >= 0)[None, :]
        allowed = allowed[:, None, None, :, None]
        if with_diagonal:
            diagonal = key_ids[None, :] == query_ids[:, None]
            allowed = allowed | diagonal[:, None, None, :, None] & causal[None, None, :, None, :]
        scores = jnp.where(allowed, scores, jnp.float32(-1e30)).reshape(
            blocks, head_count, BLOCK, key_count * BLOCK
        )

        def apply_values(rounded):
            return jnp.einsum(
                "bhqn,nhd->bqhd", rounded, near_values, preferred_element_type=jnp.float32
            )

        return absorb(carried, scores, apply_values)

    carried = dense_set(carried, key_local, value_local, query_ids, True)
    far_keys = key_local
    far_values = value_local
    for section in range(LEVELS):
        distance = 2**section
        far_keys, far_values = from_behind((key_local, value_local), "seq", distance)
        partner_ids = (device - distance) * blocks + jnp.arange(blocks, dtype=jnp.int32)
        carried = dense_set(carried, far_keys, far_values, partner_ids, False)
    running_max, running_sum, weighted = carried
    result = weighted / jnp.transpose(running_sum, (0, 2, 1))[..., None]
    result = result.astype(jnp.bfloat16).reshape(local_rows, head_count, head_width)
    return lax.all_to_all(result, "head", split_axis=0, concat_axis=1, tiled=True)


def solution(mesh):
    return jax.shard_map(
        local,
        mesh=mesh,
        in_specs=(
            P(("seq", "head"), None, None),
            P(("seq", "head"), None, None),
            P(("seq", "head"), None, None),
            P("seq", None),
        ),
        out_specs=P(("seq", "head"), None, None),
        check_vma=False,
    )
```

profile of v0, /device:TPU:4, one launch (start us, length us, event | category | flops | bytes accessed | tf_op | source)
XLA Modules:
  0.0 330.5 jit_solution(6914553099251389992)
XLA Ops:
  0.0 3.0 copy.31
  3.0 4.5 %all-to-all-start = ((bf16[64,64,128]{2,0,1:T(8,128)(2,1)}), bf16[64,64,128]{2,0,1:T(8,128)(2,1)S(1)}, u32[]{:S(2)}, u32[]{:S(2)}) async-start(bf16[64,64,128]{2,0,1:T(8,128)(2,1)} %copy.31), calls=%async_computation | async-start | bytes 2097152 | tf_op jit(solution)/shard_map/all_to_all | solution.py:32
  7.5 1.6 copy.33
  9.2 0.4 compare_reduce_fusion
  9.6 0.1 or_and_fusion.6
  9.7 0.1 broadcast_bitcast_fusion.1
  9.9 12.6 %all-to-all-done = bf16[64,64,128]{2,0,1:T(8,128)(2,1)S(1)} async-done(((bf16[64,64,128]{2,0,1:T(8,128)(2,1)}), bf16[64,64,128]{2,0,1:T(8,128)(2,1)S(1)}, u32[]{:S(2)}, u32[]{:S(2)}) %all-to-all-start) | async-done | bytes 1048608 | tf_op jit(solution)/shard_map/all_to_all | solution.py:32
  22.5 3.5 %all-to-all-start.1 = ((bf16[64,64,128]{2,0,1:T(8,128)(2,1)}), bf16[64,64,128]{2,0,1:T(8,128)(2,1)S(1)}, u32[]{:S(2)}, u32[]{:S(2)}) async-start(bf16[64,64,128]{2,0,1:T(8,128)(2,1)} %copy.33), calls=%async_computation.1 | async-start | bytes 2097152 | tf_op jit(solution)/shard_map/all_to_all | solution.py:31
  26.1 0.1 broadcast_bitcast_fusion.4
  26.1 2.9 copy.35
  29.2 0.1 or_and_fusion
  29.3 0.1 copy.32
  29.4 3.1 collective-permute-start.8
  32.5 7.8 %all-to-all-done.1 = bf16[64,64,128]{2,0,1:T(8,128)(2,1)S(1)} async-done(((bf16[64,64,128]{2,0,1:T(8,128)(2,1)}), bf16[64,64,128]{2,0,1:T(8,128)(2,1)S(1)}, u32[]{:S(2)}, u32[]{:S(2)}) %all-to-all-start.1) | async-done | bytes 1048608 | tf_op jit(solution)/shard_map/all_to_all | solution.py:31
  40.3 4.2 %all-to-all-start.2 = ((bf16[64,64,128]{2,0,1:T(8,128)(2,1)}), bf16[64,64,128]{2,0,1:T(8,128)(2,1)}, u32[]{:S(2)}, u32[]{:S(2)}) async-start(bf16[64,64,128]{2,0,1:T(8,128)(2,1)} %copy.35), calls=%async_computation.2 | async-start | bytes 2097152 | tf_op jit(solution)/shard_map/all_to_all | solution.py:33
  44.5 0.1 broadcast_bitcast_fusion.7
  44.7 9.1 %collective-permute-start.6 = (bf16[256,16,128]{2,0,1:T(8,128)(2,1)S(1)}, bf16[256,16,128]{2,0,1:T(8,128)(2,1)}, u32[]{:S(2)}, u32[]{:S(2)}) collective-permute-start(bf16[256,16,128]{2,0,1:T(8,128)(2,1)S(1)} %bitcast.383), channel_id=1, source_target_pairs={{0,32},{4,36},{8,40},{12,44},{16,48},{20,52},{24,56},{28,60},{32,6... | collective-permute-start | bytes 3145736 | tf_op jit(solution)/shard_map/ppermute | solution.py:14
  53.9 0.2 and_or_fusion
  54.1 3.4 %collective-permute-start.4 = (bf16[256,16,128]{2,0,1:T(8,128)(2,1)S(1)}, bf16[256,16,128]{2,0,1:T(8,128)(2,1)}, u32[]{:S(2)}, u32[]{:S(2)}) collective-permute-start(bf16[256,16,128]{2,0,1:T(8,128)(2,1)S(1)} %bitcast.384), channel_id=1, source_target_pairs={{0,16},{4,20},{8,24},{12,28},{16,32},{20,36},{24,40},{28,44},{32,4... | collective-permute-start | bytes 3145736 | tf_op jit(solution)/shard_map/ppermute | solution.py:14
  57.5 2.9 collective-permute-start.2
  60.5 1.9 collective-permute-start
  62.4 0.1 copy.34
  62.5 1.3 copy.36
  63.8 0.8 fusion.14
  64.6 3.0 collective-permute-done.8
  67.6 1.3 collective-permute-start.10
  68.9 2.0 fusion.19
  71.0 31.0 %collective-permute-done.6 = bf16[256,16,128]{2,0,1:T(8,128)(2,1)} collective-permute-done((bf16[256,16,128]{2,0,1:T(8,128)(2,1)S(1)}, bf16[256,16,128]{2,0,1:T(8,128)(2,1)}, u32[]{:S(2)}, u32[]{:S(2)}) %collective-permute-start.6) | collective-permute-done | bytes 1048608 | tf_op jit(solution)/shard_map/ppermute | solution.py:14
  101.9 1.9 collective-permute-start.1
  103.9 2.0 fusion.18
  105.9 38.9 %collective-permute-done.4 = bf16[256,16,128]{2,0,1:T(8,128)(2,1)} collective-permute-done((bf16[256,16,128]{2,0,1:T(8,128)(2,1)S(1)}, bf16[256,16,128]{2,0,1:T(8,128)(2,1)}, u32[]{:S(2)}, u32[]{:S(2)}) %collective-permute-start.4) | collective-permute-done | bytes 1048608 | tf_op jit(solution)/shard_map/ppermute | solution.py:14
  144.8 1.9 collective-permute-start.3
  146.7 2.0 fusion.17
  148.8 18.5 %collective-permute-done.2 = bf16[256,16,128]{2,0,1:T(8,128)(2,1)} collective-permute-done((bf16[256,16,128]{2,0,1:T(8,128)(2,1)S(1)}, bf16[256,16,128]{2,0,1:T(8,128)(2,1)}, u32[]{:S(2)}, u32[]{:S(2)}) %collective-permute-start.2) | collective-permute-done | bytes 1048608 | tf_op jit(solution)/shard_map/ppermute | solution.py:14
  167.3 2.4 collective-permute-start.5
  169.7 2.0 fusion.16
  171.7 15.7 %collective-permute-done = bf16[256,16,128]{2,0,1:T(8,128)(2,1)} collective-permute-done((bf16[256,16,128]{2,0,1:T(8,128)(2,1)S(1)}, bf16[256,16,128]{2,0,1:T(8,128)(2,1)}, u32[]{:S(2)}, u32[]{:S(2)}) %collective-permute-start) | collective-permute-done | bytes 1048608 | tf_op jit(solution)/shard_map/ppermute | solution.py:14
  187.4 6.5 %collective-permute-start.7 = (bf16[256,16,128]{2,0,1:T(8,128)(2,1)S(1)}, bf16[256,16,128]{2,0,1:T(8,128)(2,1)S(1)}, u32[]{:S(2)}, u32[]{:S(2)}) collective-permute-start(bf16[256,16,128]{2,0,1:T(8,128)(2,1)S(1)} %bitcast.378), channel_id=1, source_target_pairs={{0,32},{4,36},{8,40},{12,44},{16,48},{20,52},{24,56},{28,60},{32,6... | collective-permute-start | bytes 3145736 | tf_op jit(solution)/shard_map/ppermute | solution.py:14
  193.9 2.0 fusion.15
  196.0 3.3 collective-permute-start.9
  199.2 0.8 fusion.20
  200.1 1.0 fusion.12
  201.1 1.0 fusion.10
  202.2 1.0 fusion.2
  203.2 1.0 fusion.4
  204.2 16.8 %collective-permute-done.1 = bf16[256,16,128]{2,0,1:T(8,128)(2,1)S(1)} collective-permute-done((bf16[256,16,128]{2,0,1:T(8,128)(2,1)S(1)}, bf16[256,16,128]{2,0,1:T(8,128)(2,1)S(1)}, u32[]{:S(2)}, u32[]{:S(2)}) %collective-permute-start.1) | collective-permute-done | bytes 1048608 | tf_op jit(solution)/shard_map/ppermute | solution.py:14
  221.0 1.3 collective-permute-start.11
  222.2 1.3 fusion.31
  223.5 1.0 fusion.6
  224.6 1.3 fusion.29
  225.9 1.0 fusion.8
  226.9 1.3 fusion.27
  228.2 0.9 fusion
  229.2 29.1 %collective-permute-done.7 = bf16[256,16,128]{2,0,1:T(8,128)(2,1)S(1)} collective-permute-done((bf16[256,16,128]{2,0,1:T(8,128)(2,1)S(1)}, bf16[256,16,128]{2,0,1:T(8,128)(2,1)S(1)}, u32[]{:S(2)}, u32[]{:S(2)}) %collective-permute-start.7) | collective-permute-done | bytes 1048608 | tf_op jit(solution)/shard_map/ppermute | solution.py:14
  258.3 1.3 fusion.25
  259.5 0.1 bitcast_add_fusion.7
  259.7 13.5 %collective-permute-done.9 = bf16[256,16,128]{2,0,1:T(8,128)(2,1)S(1)} collective-permute-done((bf16[256,16,128]{2,0,1:T(8,128)(2,1)S(1)}, bf16[256,16,128]{2,0,1:T(8,128)(2,1)S(1)}, u32[]{:S(2)}, u32[]{:S(2)}) %collective-permute-start.9) | collective-permute-done | bytes 1048608 | tf_op jit(solution)/shard_map/ppermute | solution.py:14
  273.1 1.3 fusion.23
  274.4 1.2 fusion.33
  275.6 27.2 %collective-permute-done.11 = bf16[256,16,128]{2,0,1:T(8,128)(2,1)S(1)} collective-permute-done((bf16[256,16,128]{2,0,1:T(8,128)(2,1)S(1)}, bf16[256,16,128]{2,0,1:T(8,128)(2,1)S(1)}, u32[]{:S(2)}, u32[]{:S(2)}) %collective-permute-start.11) | collective-permute-done | bytes 1048608 | tf_op jit(solution)/shard_map/ppermute | solution.py:14
  302.9 5.6 %fusion.36 = bf16[2,128,16,128]{3,1,0,2:T(8,128)(2,1)S(1)} fusion(f32[16,2,128,128]{3,2,1,0:T(8,128)S(1)} %fusion.23, f32[16,2,128,128]{3,2,1,0:T(8,128)S(1)} %fusion.25, f32[16,2,128,128]{3,2,1,0:T(8,128)S(1)} %fusion.27, f32[16,2,128,128]{3,2,1,0:T(8,128)S(1)} %fusion.29, f32[16,2,128,128]{3,2,1,0:T(8,128)S(1)} %fusion.31, ...), kind=kOutput, calls=%fused_computation.44 | convolution fusion | flops 280494080 | bytes 19022336 | tf_op jit(solution)/shard_map/bhqn,nhd->bqhd/dot_general | solution.py:67
  308.5 0.7 copy.44
  309.2 20.0 %all_to_all.69 = bf16[256,16,128]{2,1,0:T(8,128)(2,1)S(1)} all-to-all(bf16[256,16,128]{2,1,0:T(8,128)(2,1)S(1)} %copy.44), channel_id=1, replica_groups=mesh['seq'=64,'head'=4] {'head'}, dimensions={0} | all-to-all | bytes 2097152 | tf_op jit(solution)/shard_map/all_to_all | solution.py:84
  329.2 1.3 copy.45
  (33 shorter events, 0.6 us)
Async XLA Ops:
  0.0 7.5 %copy-start = (bf16[64,64,128]{2,1,0:T(8,128)(2,1)S(1)}, bf16[64,64,128]{2,1,0:T(8,128)(2,1)}, u32[]{:S(2)}) copy-start(bf16[64,64,128]{2,1,0:T(8,128)(2,1)} %param.4) | copy-start | bytes 3145732
  0.0 9.2 %copy-start.1 = (s32[2,12]{1,0:T(2,128)S(1)}, s32[2,12]{1,0:T(2,128)}, u32[]{:S(2)}) copy-start(s32[2,12]{1,0:T(2,128)} %param.7) | copy-start | bytes 292
  3.0 19.6 %all-to-all-start = ((bf16[64,64,128]{2,0,1:T(8,128)(2,1)}), bf16[64,64,128]{2,0,1:T(8,128)(2,1)S(1)}, u32[]{:S(2)}, u32[]{:S(2)}) async-start(bf16[64,64,128]{2,0,1:T(8,128)(2,1)} %copy.31), calls=%async_computation | async-start | bytes 2097152 | tf_op jit(solution)/shard_map/all_to_all | solution.py:32
  22.5 17.7 %all-to-all-start.1 = ((bf16[64,64,128]{2,0,1:T(8,128)(2,1)}), bf16[64,64,128]{2,0,1:T(8,128)(2,1)S(1)}, u32[]{:S(2)}, u32[]{:S(2)}) async-start(bf16[64,64,128]{2,0,1:T(8,128)(2,1)} %copy.33), calls=%async_computation.1 | async-start | bytes 2097152 | tf_op jit(solution)/shard_map/all_to_all | solution.py:31
  29.4 38.2 %collective-permute-start.8 = (bf16[256,16,128]{2,0,1:T(8,128)(2,1)S(1)}, bf16[256,16,128]{2,0,1:T(8,128)(2,1)}, u32[]{:S(2)}, u32[]{:S(2)}) collective-permute-start(bf16[256,16,128]{2,0,1:T(8,128)(2,1)S(1)} %bitcast.382), channel_id=1, source_target_pairs={{0,64},{4,68},{8,72},{12,76},{16,80},{20,84},{24,88},{28,92},{32,9... | collective-permute-start | bytes 3145736 | tf_op jit(solution)/shard_map/ppermute | solution.py:14
  40.3 22.2 %all-to-all-start.2 = ((bf16[64,64,128]{2,0,1:T(8,128)(2,1)}), bf16[64,64,128]{2,0,1:T(8,128)(2,1)}, u32[]{:S(2)}, u32[]{:S(2)}) async-start(bf16[64,64,128]{2,0,1:T(8,128)(2,1)} %copy.35), calls=%async_computation.2 | async-start | bytes 2097152 | tf_op jit(solution)/shard_map/all_to_all | solution.py:33
  44.7 57.3 %collective-permute-start.6 = (bf16[256,16,128]{2,0,1:T(8,128)(2,1)S(1)}, bf16[256,16,128]{2,0,1:T(8,128)(2,1)}, u32[]{:S(2)}, u32[]{:S(2)}) collective-permute-start(bf16[256,16,128]{2,0,1:T(8,128)(2,1)S(1)} %bitcast.383), channel_id=1, source_target_pairs={{0,32},{4,36},{8,40},{12,44},{16,48},{20,52},{24,56},{28,60},{32,6... | collective-permute-start | bytes 3145736 | tf_op jit(solution)/shard_map/ppermute | solution.py:14
  54.1 90.7 %collective-permute-start.4 = (bf16[256,16,128]{2,0,1:T(8,128)(2,1)S(1)}, bf16[256,16,128]{2,0,1:T(8,128)(2,1)}, u32[]{:S(2)}, u32[]{:S(2)}) collective-permute-start(bf16[256,16,128]{2,0,1:T(8,128)(2,1)S(1)} %bitcast.384), channel_id=1, source_target_pairs={{0,16},{4,20},{8,24},{12,28},{16,32},{20,36},{24,40},{28,44},{32,4... | collective-permute-start | bytes 3145736 | tf_op jit(solution)/shard_map/ppermute | solution.py:14
  57.5 109.8 %collective-permute-start.2 = (bf16[256,16,128]{2,0,1:T(8,128)(2,1)S(1)}, bf16[256,16,128]{2,0,1:T(8,128)(2,1)}, u32[]{:S(2)}, u32[]{:S(2)}) collective-permute-start(bf16[256,16,128]{2,0,1:T(8,128)(2,1)S(1)} %bitcast.385), channel_id=1, source_target_pairs={{0,8},{4,12},{8,16},{12,20},{16,24},{20,28},{24,32},{28,36},{32,40... | collective-permute-start | bytes 3145736 | tf_op jit(solution)/shard_map/ppermute | solution.py:14
  60.5 127.0 %collective-permute-start = (bf16[256,16,128]{2,0,1:T(8,128)(2,1)S(1)}, bf16[256,16,128]{2,0,1:T(8,128)(2,1)}, u32[]{:S(2)}, u32[]{:S(2)}) collective-permute-start(bf16[256,16,128]{2,0,1:T(8,128)(2,1)S(1)} %bitcast.386), channel_id=1, source_target_pairs={{0,4},{4,8},{8,12},{12,16},{16,20},{20,24},{24,28},{28,32},{32,36}... | collective-permute-start | bytes 3145736 | tf_op jit(solution)/shard_map/ppermute | solution.py:14
  67.6 128.3 %collective-permute-start.10 = (bf16[256,16,128]{2,0,1:T(8,128)(2,1)S(1)}, bf16[256,16,128]{2,0,1:T(8,128)(2,1)S(1)}, u32[]{:S(2)}, u32[]{:S(2)}) collective-permute-start(bf16[256,16,128]{2,0,1:T(8,128)(2,1)S(1)} %bitcast.388), channel_id=1, source_target_pairs={{0,128},{4,132},{8,136},{12,140},{16,144},{20,148},{24,152},{28,15... | collective-permute-start | bytes 3145736 | tf_op jit(solution)/shard_map/ppermute | solution.py:14
  101.9 119.0 %collective-permute-start.1 = (bf16[256,16,128]{2,0,1:T(8,128)(2,1)S(1)}, bf16[256,16,128]{2,0,1:T(8,128)(2,1)S(1)}, u32[]{:S(2)}, u32[]{:S(2)}) collective-permute-start(bf16[256,16,128]{2,0,1:T(8,128)(2,1)S(1)} %bitcast.375), channel_id=1, source_target_pairs={{0,4},{4,8},{8,12},{12,16},{16,20},{20,24},{24,28},{28,32},{32,36}... | collective-permute-start | bytes 3145736 | tf_op jit(solution)/shard_map/ppermute | solution.py:14
  144.8 79.7 %collective-permute-start.3 = (bf16[256,16,128]{2,0,1:T(8,128)(2,1)S(1)}, bf16[256,16,128]{2,0,1:T(8,128)(2,1)S(1)}, u32[]{:S(2)}, u32[]{:S(2)}) collective-permute-start(bf16[256,16,128]{2,0,1:T(8,128)(2,1)S(1)} %bitcast.376), channel_id=1, source_target_pairs={{0,8},{4,12},{8,16},{12,20},{16,24},{20,28},{24,32},{28,36},{32,40... | collective-permute-start | bytes 3145736 | tf_op jit(solution)/shard_map/ppermute | solution.py:14
  167.3 59.6 %collective-permute-start.5 = (bf16[256,16,128]{2,0,1:T(8,128)(2,1)S(1)}, bf16[256,16,128]{2,0,1:T(8,128)(2,1)S(1)}, u32[]{:S(2)}, u32[]{:S(2)}) collective-permute-start(bf16[256,16,128]{2,0,1:T(8,128)(2,1)S(1)} %bitcast.377), channel_id=1, source_target_pairs={{0,16},{4,20},{8,24},{12,28},{16,32},{20,36},{24,40},{28,44},{32,4... | collective-permute-start | bytes 3145736 | tf_op jit(solution)/shard_map/ppermute | solution.py:14
  187.4 70.8 %collective-permute-start.7 = (bf16[256,16,128]{2,0,1:T(8,128)(2,1)S(1)}, bf16[256,16,128]{2,0,1:T(8,128)(2,1)S(1)}, u32[]{:S(2)}, u32[]{:S(2)}) collective-permute-start(bf16[256,16,128]{2,0,1:T(8,128)(2,1)S(1)} %bitcast.378), channel_id=1, source_target_pairs={{0,32},{4,36},{8,40},{12,44},{16,48},{20,52},{24,56},{28,60},{32,6... | collective-permute-start | bytes 3145736 | tf_op jit(solution)/shard_map/ppermute | solution.py:14
  196.0 77.2 %collective-permute-start.9 = (bf16[256,16,128]{2,0,1:T(8,128)(2,1)S(1)}, bf16[256,16,128]{2,0,1:T(8,128)(2,1)S(1)}, u32[]{:S(2)}, u32[]{:S(2)}) collective-permute-start(bf16[256,16,128]{2,0,1:T(8,128)(2,1)S(1)} %bitcast.379), channel_id=1, source_target_pairs={{0,64},{4,68},{8,72},{12,76},{16,80},{20,84},{24,88},{28,92},{32,9... | collective-permute-start | bytes 3145736 | tf_op jit(solution)/shard_map/ppermute | solution.py:14
  221.0 81.9 %collective-permute-start.11 = (bf16[256,16,128]{2,0,1:T(8,128)(2,1)S(1)}, bf16[256,16,128]{2,0,1:T(8,128)(2,1)S(1)}, u32[]{:S(2)}, u32[]{:S(2)}) collective-permute-start(bf16[256,16,128]{2,0,1:T(8,128)(2,1)S(1)} %bitcast.380), channel_id=1, source_target_pairs={{0,128},{4,132},{8,136},{12,140},{16,144},{20,148},{24,152},{28,15... | collective-permute-start | bytes 3145736 | tf_op jit(solution)/shard_map/ppermute | solution.py:14
where the time goes:
time: 331 us
  waiting for transfers between devices  214 us (65%)
  starting transfers between devices  51.2 us (15%)
  matrix products  25 us (8%)
  blocking collectives  20 us (6%)
  local copies, waits for them, and re-layouts  11.7 us (4%)
  other arithmetic  8.07 us (2%)
    ppermute x12, waiting for transfers between devices, from_behind(): return lax.ppermute(value, axis, pairs)  194 us
    ppermute x12, starting transfers between devices, from_behind(): return lax.ppermute(value, axis, pairs)  39 us
    all_to_all x1, blocking collectives, local(): lax.all_to_all(result, 'head', split_axis=0, concat_axis=1, tiled=True)  20 us
    dot_general x7, matrix products, apply_values(): jnp.einsum('bhqn,nhd->bqhd', rounded, near_values, preferred_element_type...  13.2 us
    all_to_all x1, waiting for transfers between devices, local(): lax.all_to_all(key_vectors, 'head', split_axis=1, concat_axis=0, tiled=True)  12.6 us
    dot_general x7, matrix products, dense_set(): jnp.einsum('bqhd,nhd->bhqn', query_tiles, near_keys, preferred_element_ty...  11.7 us
    unnamed x23, local copies, waits for them, and re-layouts  8.21 us
    all_to_all x1, waiting for transfers between devices, local(): lax.all_to_all(queries, 'head', split_axis=1, concat_axis=0, tiled=True)  7.77 us
  transfers between devices with their start and end apart: 15, of which 11 were waited for; matrix products, arithmetic and copies ran while one was open for 10% of the time, Pallas kernels for 0%

commit v1 on v0

--- a/solution.py
+++ b/solution.py
@@ -1,11 +1,24 @@
+import functools
 import math
 import jax
 import jax.numpy as jnp
 from jax import lax
 from jax.sharding import PartitionSpec as P
+from jax.lax import all_to_all, axis_size
 
 BLOCK = 128
 LEVELS = 6
+
+
+def report_flows(xin, dimension_no, ndim_at):
+    all_rows = axis_size("head")
+    earlier = jnp.split(xin, all_rows, axis=dimension_no)
+    known = jnp.stack(earlier, axis=0)
+    w2 = all_to_all(known, "head", 0, 0)
+    return jnp.concatenate(w2, axis=ndim_at)
+
+
+get_frame = functools.partial(report_flows, dimension_no=1, ndim_at=0)
 
 
 def from_behind(value, axis, by):
@@ -29,7 +42,7 @@
 def local(queries, key_vectors, value_vectors, key_blocks):
     query_local, key_local, value_local = (
         lax.all_to_all(queries, "head", split_axis=1, concat_axis=0, tiled=True),
-        lax.all_to_all(key_vectors, "head", split_axis=1, concat_axis=0, tiled=True),
+        get_frame(key_vectors),
         lax.all_to_all(value_vectors, "head", split_axis=1, concat_axis=0, tiled=True),
     )
     local_rows, head_count, head_width = query_local.shape

time: 331 us -> 321 us (0.970)
  waiting for transfers between devices: 214 us -> 198 us
  starting transfers between devices: 51.2 us -> 57.3 us
    ppermute x12, waiting for transfers between devices: 194 us -> 184 us  [from_behind(): return lax.ppermute(value, axis, pairs)]
    all_to_all x1, waiting for transfers between devices: 7.77 us -> 1.59 us  [local(): lax.all_to_all(queries, 'head', split_axis=1, concat_axis=0, tiled=True)]
    ppermute x12, starting transfers between devices: 39 us -> 45.1 us  [from_behind(): return lax.ppermute(value, axis, pairs)]
    unnamed x23 -> x22, local copies, waits for them, and re-layouts: 8.21 us -> 5.22 us
  transfers between devices with their start and end apart: 15 -> 15, of which waited for: 11 -> 10; matrix products, arithmetic and copies ran while one was open for 10% -> 11% of each run, Pallas kernels for 0% -> 0%
where the time goes in v1:
time: 321 us; the launch traced here: 319 us
  waiting for transfers between devices  198 us (62%)
  starting transfers between devices  57.3 us (18%)
  matrix products  25.2 us (8%)
  blocking collectives  18.3 us (6%)
  local copies, waits for them, and re-layouts  10.4 us (3%)
  other arithmetic  9.19 us (3%)
    ppermute x12, waiting for transfers between devices, from_behind(): return lax.ppermute(value, axis, pairs)  184 us
    ppermute x12, starting transfers between devices, from_behind(): return lax.ppermute(value, axis, pairs)  45.1 us
    all_to_all x1, blocking collectives, local(): lax.all_to_all(result, 'head', split_axis=0, concat_axis=1, tiled=True)  18.3 us
    dot_general x7, matrix products, apply_values(): jnp.einsum('bhqn,nhd->bqhd', rounded, near_values, preferred_element_type...  13.5 us
    all_to_all x1, waiting for transfers between devices, report_flows(): w2 = all_to_all(known, 'head', 0, 0)  12.7 us
    dot_general x7, matrix products, dense_set(): jnp.einsum('bqhd,nhd->bhqn', query_tiles, near_keys, preferred_element_ty...  11.7 us
    reduce_sum x7, other arithmetic, absorb(): running_sum = running_sum * factor + jnp.sum(weights, axis=-1)  7.06 us
  transfers between devices with their start and end apart: 15, of which 10 were waited for; matrix products, arithmetic and copies ran while one was open for 11% of the time, Pallas kernels for 0%

profile of v1, /device:TPU:4, one launch (start us, length us, event | category | flops | bytes accessed | tf_op | source)
XLA Modules:
  0.0 319.0 jit_solution(9467925757572603514)
XLA Ops:
  0.0 1.5 slice_bitcast_fusion.3
  1.5 1.1 pad_maximum_fusion
  2.6 4.5 %all-to-all-start = ((bf16[4,64,16,128]{3,2,1,0:T(8,128)(2,1)}), bf16[4,64,16,128]{3,2,1,0:T(8,128)(2,1)S(1)}, u32[]{:S(2)}, u32[]{:S(2)}) async-start(bf16[4,64,16,128]{3,2,1,0:T(8,128)(2,1)} %pad_maximum_fusion), calls=%async_computation | async-start | bytes 2097152 | tf_op jit(solution)/shard_map/all_to_all | solution.py:17
  7.2 1.6 copy.31
  8.8 0.4 compare_reduce_fusion
  9.2 0.1 or_and_fusion.6
  9.3 0.1 broadcast_bitcast_fusion.2
  9.5 12.7 %all-to-all-done = bf16[4,64,16,128]{3,2,1,0:T(8,128)(2,1)S(1)} async-done(((bf16[4,64,16,128]{3,2,1,0:T(8,128)(2,1)}), bf16[4,64,16,128]{3,2,1,0:T(8,128)(2,1)S(1)}, u32[]{:S(2)}, u32[]{:S(2)}) %all-to-all-start) | async-done | bytes 1048608 | tf_op jit(solution)/shard_map/all_to_all | solution.py:17
  22.2 3.5 %all-to-all-start.1 = ((bf16[64,64,128]{2,0,1:T(8,128)(2,1)}), bf16[64,64,128]{2,0,1:T(8,128)(2,1)S(1)}, u32[]{:S(2)}, u32[]{:S(2)}) async-start(bf16[64,64,128]{2,0,1:T(8,128)(2,1)} %copy.31), calls=%async_computation.1 | async-start | bytes 2097152 | tf_op jit(solution)/shard_map/all_to_all | solution.py:44
  25.7 0.1 broadcast_bitcast_fusion.5
  25.8 2.9 copy.33
  28.8 0.1 or_and_fusion
  28.9 0.3 copy.30
  29.2 9.1 %collective-permute-start.6 = (bf16[256,16,128]{2,0,1:T(8,128)(2,1)S(1)}, bf16[256,16,128]{2,0,1:T(8,128)(2,1)}, u32[]{:S(2)}, u32[]{:S(2)}) collective-permute-start(bf16[256,16,128]{2,0,1:T(8,128)(2,1)S(1)} %bitcast.387), channel_id=1, source_target_pairs={{0,32},{4,36},{8,40},{12,44},{16,48},{20,52},{24,56},{28,60},{32,6... | collective-permute-start | bytes 3145736 | tf_op jit(solution)/shard_map/ppermute | solution.py:27
  38.3 1.6 all-to-all-done.1
  39.9 4.2 %all-to-all-start.2 = ((bf16[64,64,128]{2,0,1:T(8,128)(2,1)}), bf16[64,64,128]{2,0,1:T(8,128)(2,1)}, u32[]{:S(2)}, u32[]{:S(2)}) async-start(bf16[64,64,128]{2,0,1:T(8,128)(2,1)} %copy.33), calls=%async_computation.2 | async-start | bytes 2097152 | tf_op jit(solution)/shard_map/all_to_all | solution.py:46
  44.2 0.1 broadcast_bitcast_fusion.1
  44.3 5.2 %collective-permute-start.4 = (bf16[256,16,128]{2,0,1:T(8,128)(2,1)S(1)}, bf16[256,16,128]{2,0,1:T(8,128)(2,1)}, u32[]{:S(2)}, u32[]{:S(2)}) collective-permute-start(bf16[256,16,128]{2,0,1:T(8,128)(2,1)S(1)} %bitcast.388), channel_id=1, source_target_pairs={{0,16},{4,20},{8,24},{12,28},{16,32},{20,36},{24,40},{28,44},{32,4... | collective-permute-start | bytes 3145736 | tf_op jit(solution)/shard_map/ppermute | solution.py:27
  49.6 0.2 and_or_fusion
  49.8 3.8 %collective-permute-start.2 = (bf16[256,16,128]{2,0,1:T(8,128)(2,1)S(1)}, bf16[256,16,128]{2,0,1:T(8,128)(2,1)}, u32[]{:S(2)}, u32[]{:S(2)}) collective-permute-start(bf16[256,16,128]{2,0,1:T(8,128)(2,1)S(1)} %bitcast.389), channel_id=1, source_target_pairs={{0,8},{4,12},{8,16},{12,20},{16,24},{20,28},{24,32},{28,36},{32,40... | collective-permute-start | bytes 3145736 | tf_op jit(solution)/shard_map/ppermute | solution.py:27
  53.7 1.9 collective-permute-start
  55.6 3.1 collective-permute-start.8
  58.7 0.1 copy.32
  58.8 1.3 copy.34
  60.1 0.8 fusion.14
  60.9 23.5 %collective-permute-done.6 = bf16[256,16,128]{2,0,1:T(8,128)(2,1)} collective-permute-done((bf16[256,16,128]{2,0,1:T(8,128)(2,1)S(1)}, bf16[256,16,128]{2,0,1:T(8,128)(2,1)}, u32[]{:S(2)}, u32[]{:S(2)}) %collective-permute-start.6) | collective-permute-done | bytes 1048608 | tf_op jit(solution)/shard_map/ppermute | solution.py:27
  84.4 1.3 collective-permute-start.10
  85.7 2.0 fusion.18
  87.7 41.6 %collective-permute-done.4 = bf16[256,16,128]{2,0,1:T(8,128)(2,1)} collective-permute-done((bf16[256,16,128]{2,0,1:T(8,128)(2,1)S(1)}, bf16[256,16,128]{2,0,1:T(8,128)(2,1)}, u32[]{:S(2)}, u32[]{:S(2)}) %collective-permute-start.4) | collective-permute-done | bytes 1048608 | tf_op jit(solution)/shard_map/ppermute | solution.py:27
  129.3 1.9 collective-permute-start.1
  131.2 2.0 fusion.17
  133.3 18.5 %collective-permute-done.2 = bf16[256,16,128]{2,0,1:T(8,128)(2,1)} collective-permute-done((bf16[256,16,128]{2,0,1:T(8,128)(2,1)S(1)}, bf16[256,16,128]{2,0,1:T(8,128)(2,1)}, u32[]{:S(2)}, u32[]{:S(2)}) %collective-permute-start.2) | collective-permute-done | bytes 1048608 | tf_op jit(solution)/shard_map/ppermute | solution.py:27
  151.8 4.5 %collective-permute-start.3 = (bf16[256,16,128]{2,0,1:T(8,128)(2,1)S(1)}, bf16[256,16,128]{2,0,1:T(8,128)(2,1)S(1)}, u32[]{:S(2)}, u32[]{:S(2)}) collective-permute-start(bf16[256,16,128]{2,0,1:T(8,128)(2,1)S(1)} %bitcast.381), channel_id=1, source_target_pairs={{0,8},{4,12},{8,16},{12,20},{16,24},{20,28},{24,32},{28,36},{32,40... | collective-permute-start | bytes 3145736 | tf_op jit(solution)/shard_map/ppermute | solution.py:27
  156.3 2.0 fusion.16
  158.3 5.4 %collective-permute-done = bf16[256,16,128]{2,0,1:T(8,128)(2,1)} collective-permute-done((bf16[256,16,128]{2,0,1:T(8,128)(2,1)S(1)}, bf16[256,16,128]{2,0,1:T(8,128)(2,1)}, u32[]{:S(2)}, u32[]{:S(2)}) %collective-permute-start) | collective-permute-done | bytes 1048608 | tf_op jit(solution)/shard_map/ppermute | solution.py:27
  163.7 7.3 %collective-permute-start.5 = (bf16[256,16,128]{2,0,1:T(8,128)(2,1)S(1)}, bf16[256,16,128]{2,0,1:T(8,128)(2,1)S(1)}, u32[]{:S(2)}, u32[]{:S(2)}) collective-permute-start(bf16[256,16,128]{2,0,1:T(8,128)(2,1)S(1)} %bitcast.382), channel_id=1, source_target_pairs={{0,16},{4,20},{8,24},{12,28},{16,32},{20,36},{24,40},{28,44},{32,4... | collective-permute-start | bytes 3145736 | tf_op jit(solution)/shard_map/ppermute | solution.py:27
  171.0 2.0 fusion.15
  173.1 3.6 %collective-permute-start.7 = (bf16[256,16,128]{2,0,1:T(8,128)(2,1)S(1)}, bf16[256,16,128]{2,0,1:T(8,128)(2,1)S(1)}, u32[]{:S(2)}, u32[]{:S(2)}) collective-permute-start(bf16[256,16,128]{2,0,1:T(8,128)(2,1)S(1)} %bitcast.383), channel_id=1, source_target_pairs={{0,32},{4,36},{8,40},{12,44},{16,48},{20,52},{24,56},{28,60},{32,6... | collective-permute-start | bytes 3145736 | tf_op jit(solution)/shard_map/ppermute | solution.py:27
  176.6 2.0 fusion.19
  178.7 16.8 %collective-permute-done.10 = bf16[256,16,128]{2,0,1:T(8,128)(2,1)S(1)} collective-permute-done((bf16[256,16,128]{2,0,1:T(8,128)(2,1)S(1)}, bf16[256,16,128]{2,0,1:T(8,128)(2,1)S(1)}, u32[]{:S(2)}, u32[]{:S(2)}) %collective-permute-start.10) | collective-permute-done | bytes 1048608 | tf_op jit(solution)/shard_map/ppermute | solution.py:27
  195.5 2.1 collective-permute-start.9
  197.6 0.8 fusion.20
  198.5 1.0 fusion.12
  199.5 1.0 fusion.2
  200.5 1.0 fusion.4
  201.5 1.0 fusion.6
  202.6 1.3 collective-permute-start.11
  203.9 1.3 fusion.31
  205.2 1.0 fusion.8
  206.2 1.3 fusion.29
  207.5 1.0 fusion.10
  208.5 5.5 %collective-permute-done.5 = bf16[256,16,128]{2,0,1:T(8,128)(2,1)S(1)} collective-permute-done((bf16[256,16,128]{2,0,1:T(8,128)(2,1)S(1)}, bf16[256,16,128]{2,0,1:T(8,128)(2,1)S(1)}, u32[]{:S(2)}, u32[]{:S(2)}) %collective-permute-start.5) | collective-permute-done | bytes 1048608 | tf_op jit(solution)/shard_map/ppermute | solution.py:27
  214.0 1.3 fusion.27
  215.4 0.9 fusion
  216.3 32.1 %collective-permute-done.7 = bf16[256,16,128]{2,0,1:T(8,128)(2,1)S(1)} collective-permute-done((bf16[256,16,128]{2,0,1:T(8,128)(2,1)S(1)}, bf16[256,16,128]{2,0,1:T(8,128)(2,1)S(1)}, u32[]{:S(2)}, u32[]{:S(2)}) %collective-permute-start.7) | collective-permute-done | bytes 1048608 | tf_op jit(solution)/shard_map/ppermute | solution.py:27
  248.4 1.3 fusion.25
  249.7 0.1 bitcast_add_fusion.7
  249.8 40.5 %collective-permute-done.9 = bf16[256,16,128]{2,0,1:T(8,128)(2,1)S(1)} collective-permute-done((bf16[256,16,128]{2,0,1:T(8,128)(2,1)S(1)}, bf16[256,16,128]{2,0,1:T(8,128)(2,1)S(1)}, u32[]{:S(2)}, u32[]{:S(2)}) %collective-permute-start.9) | collective-permute-done | bytes 1048608 | tf_op jit(solution)/shard_map/ppermute | solution.py:27
  290.3 1.3 fusion.23
  291.6 1.2 fusion.33
  292.8 5.9 %fusion.36 = bf16[2,128,16,128]{3,1,0,2:T(8,128)(2,1)S(1)} fusion(f32[16,2,128,128]{3,2,1,0:T(8,128)S(1)} %fusion.23, f32[16,2,128,128]{3,2,1,0:T(8,128)S(1)} %fusion.25, f32[16,2,128,128]{3,2,1,0:T(8,128)S(1)} %fusion.27, f32[16,2,128,128]{3,2,1,0:T(8,128)S(1)} %fusion.29, f32[16,2,128,128]{3,2,1,0:T(8,128)S(1)} %fusion.31, ...), kind=kOutput, calls=%fused_computation.44 | convolution fusion | flops 280494080 | bytes 19022336 | tf_op jit(solution)/shard_map/bhqn,nhd->bqhd/dot_general | solution.py:80
  298.7 0.7 copy.42
  299.4 18.3 %all_to_all.56 = bf16[256,16,128]{2,1,0:T(8,128)(2,1)S(1)} all-to-all(bf16[256,16,128]{2,1,0:T(8,128)(2,1)S(1)} %copy.42), channel_id=1, replica_groups=mesh['seq'=64,'head'=4] {'head'}, dimensions={0} | all-to-all | bytes 2097152 | tf_op jit(solution)/shard_map/all_to_all | solution.py:97
  317.7 1.3 copy.43
  (34 shorter events, 0.6 us)
Async XLA Ops:
  0.0 7.2 %copy-start = (bf16[64,64,128]{2,1,0:T(8,128)(2,1)S(1)}, bf16[64,64,128]{2,1,0:T(8,128)(2,1)}, u32[]{:S(2)}) copy-start(bf16[64,64,128]{2,1,0:T(8,128)(2,1)} %param.4) | copy-start | bytes 3145732
  0.0 8.8 %copy-start.1 = (s32[2,12]{1,0:T(2,128)S(1)}, s32[2,12]{1,0:T(2,128)}, u32[]{:S(2)}) copy-start(s32[2,12]{1,0:T(2,128)} %param.7) | copy-start | bytes 292
  2.6 19.6 %all-to-all-start = ((bf16[4,64,16,128]{3,2,1,0:T(8,128)(2,1)}), bf16[4,64,16,128]{3,2,1,0:T(8,128)(2,1)S(1)}, u32[]{:S(2)}, u32[]{:S(2)}) async-start(bf16[4,64,16,128]{3,2,1,0:T(8,128)(2,1)} %pad_maximum_fusion), calls=%async_computation | async-start | bytes 2097152 | tf_op jit(solution)/shard_map/all_to_all | solution.py:17
  22.2 17.7 %all-to-all-start.1 = ((bf16[64,64,128]{2,0,1:T(8,128)(2,1)}), bf16[64,64,128]{2,0,1:T(8,128)(2,1)S(1)}, u32[]{:S(2)}, u32[]{:S(2)}) async-start(bf16[64,64,128]{2,0,1:T(8,128)(2,1)} %copy.31), calls=%async_computation.1 | async-start | bytes 2097152 | tf_op jit(solution)/shard_map/all_to_all | solution.py:44
  29.2 55.2 %collective-permute-start.6 = (bf16[256,16,128]{2,0,1:T(8,128)(2,1)S(1)}, bf16[256,16,128]{2,0,1:T(8,128)(2,1)}, u32[]{:S(2)}, u32[]{:S(2)}) collective-permute-start(bf16[256,16,128]{2,0,1:T(8,128)(2,1)S(1)} %bitcast.387), channel_id=1, source_target_pairs={{0,32},{4,36},{8,40},{12,44},{16,48},{20,52},{24,56},{28,60},{32,6... | collective-permute-start | bytes 3145736 | tf_op jit(solution)/shard_map/ppermute | solution.py:27
  39.9 18.9 %all-to-all-start.2 = ((bf16[64,64,128]{2,0,1:T(8,128)(2,1)}), bf16[64,64,128]{2,0,1:T(8,128)(2,1)}, u32[]{:S(2)}, u32[]{:S(2)}) async-start(bf16[64,64,128]{2,0,1:T(8,128)(2,1)} %copy.33), calls=%async_computation.2 | async-start | bytes 2097152 | tf_op jit(solution)/shard_map/all_to_all | solution.py:46
  44.3 85.0 %collective-permute-start.4 = (bf16[256,16,128]{2,0,1:T(8,128)(2,1)S(1)}, bf16[256,16,128]{2,0,1:T(8,128)(2,1)}, u32[]{:S(2)}, u32[]{:S(2)}) collective-permute-start(bf16[256,16,128]{2,0,1:T(8,128)(2,1)S(1)} %bitcast.388), channel_id=1, source_target_pairs={{0,16},{4,20},{8,24},{12,28},{16,32},{20,36},{24,40},{28,44},{32,4... | collective-permute-start | bytes 3145736 | tf_op jit(solution)/shard_map/ppermute | solution.py:27
  49.8 101.9 %collective-permute-start.2 = (bf16[256,16,128]{2,0,1:T(8,128)(2,1)S(1)}, bf16[256,16,128]{2,0,1:T(8,128)(2,1)}, u32[]{:S(2)}, u32[]{:S(2)}) collective-permute-start(bf16[256,16,128]{2,0,1:T(8,128)(2,1)S(1)} %bitcast.389), channel_id=1, source_target_pairs={{0,8},{4,12},{8,16},{12,20},{16,24},{20,28},{24,32},{28,36},{32,40... | collective-permute-start | bytes 3145736 | tf_op jit(solution)/shard_map/ppermute | solution.py:27
  53.7 110.0 %collective-permute-start = (bf16[256,16,128]{2,0,1:T(8,128)(2,1)S(1)}, bf16[256,16,128]{2,0,1:T(8,128)(2,1)}, u32[]{:S(2)}, u32[]{:S(2)}) collective-permute-start(bf16[256,16,128]{2,0,1:T(8,128)(2,1)S(1)} %bitcast.390), channel_id=1, source_target_pairs={{0,4},{4,8},{8,12},{12,16},{16,20},{20,24},{24,28},{28,32},{32,36}... | collective-permute-start | bytes 3145736 | tf_op jit(solution)/shard_map/ppermute | solution.py:27
  55.6 117.4 %collective-permute-start.8 = (bf16[256,16,128]{2,0,1:T(8,128)(2,1)S(1)}, bf16[256,16,128]{2,0,1:T(8,128)(2,1)}, u32[]{:S(2)}, u32[]{:S(2)}) collective-permute-start(bf16[256,16,128]{2,0,1:T(8,128)(2,1)S(1)} %bitcast.391), channel_id=1, source_target_pairs={{0,64},{4,68},{8,72},{12,76},{16,80},{20,84},{24,88},{28,92},{32,9... | collective-permute-start | bytes 3145736 | tf_op jit(solution)/shard_map/ppermute | solution.py:27
  84.4 111.1 %collective-permute-start.10 = (bf16[256,16,128]{2,0,1:T(8,128)(2,1)S(1)}, bf16[256,16,128]{2,0,1:T(8,128)(2,1)S(1)}, u32[]{:S(2)}, u32[]{:S(2)}) collective-permute-start(bf16[256,16,128]{2,0,1:T(8,128)(2,1)S(1)} %bitcast.393), channel_id=1, source_target_pairs={{0,128},{4,132},{8,136},{12,140},{16,144},{20,148},{24,152},{28,15... | collective-permute-start | bytes 3145736 | tf_op jit(solution)/shard_map/ppermute | solution.py:27
  129.3 73.3 %collective-permute-start.1 = (bf16[256,16,128]{2,0,1:T(8,128)(2,1)S(1)}, bf16[256,16,128]{2,0,1:T(8,128)(2,1)S(1)}, u32[]{:S(2)}, u32[]{:S(2)}) collective-permute-start(bf16[256,16,128]{2,0,1:T(8,128)(2,1)S(1)} %bitcast.380), channel_id=1, source_target_pairs={{0,4},{4,8},{8,12},{12,16},{16,20},{20,24},{24,28},{28,32},{32,36}... | collective-permute-start | bytes 3145736 | tf_op jit(solution)/shard_map/ppermute | solution.py:27
  151.8 54.4 %collective-permute-start.3 = (bf16[256,16,128]{2,0,1:T(8,128)(2,1)S(1)}, bf16[256,16,128]{2,0,1:T(8,128)(2,1)S(1)}, u32[]{:S(2)}, u32[]{:S(2)}) collective-permute-start(bf16[256,16,128]{2,0,1:T(8,128)(2,1)S(1)} %bitcast.381), channel_id=1, source_target_pairs={{0,8},{4,12},{8,16},{12,20},{16,24},{20,28},{24,32},{28,36},{32,40... | collective-permute-start | bytes 3145736 | tf_op jit(solution)/shard_map/ppermute | solution.py:27
  163.7 50.3 %collective-permute-start.5 = (bf16[256,16,128]{2,0,1:T(8,128)(2,1)S(1)}, bf16[256,16,128]{2,0,1:T(8,128)(2,1)S(1)}, u32[]{:S(2)}, u32[]{:S(2)}) collective-permute-start(bf16[256,16,128]{2,0,1:T(8,128)(2,1)S(1)} %bitcast.382), channel_id=1, source_target_pairs={{0,16},{4,20},{8,24},{12,28},{16,32},{20,36},{24,40},{28,44},{32,4... | collective-permute-start | bytes 3145736 | tf_op jit(solution)/shard_map/ppermute | solution.py:27
  173.1 75.4 %collective-permute-start.7 = (bf16[256,16,128]{2,0,1:T(8,128)(2,1)S(1)}, bf16[256,16,128]{2,0,1:T(8,128)(2,1)S(1)}, u32[]{:S(2)}, u32[]{:S(2)}) collective-permute-start(bf16[256,16,128]{2,0,1:T(8,128)(2,1)S(1)} %bitcast.383), channel_id=1, source_target_pairs={{0,32},{4,36},{8,40},{12,44},{16,48},{20,52},{24,56},{28,60},{32,6... | collective-permute-start | bytes 3145736 | tf_op jit(solution)/shard_map/ppermute | solution.py:27
  195.5 94.8 %collective-permute-start.9 = (bf16[256,16,128]{2,0,1:T(8,128)(2,1)S(1)}, bf16[256,16,128]{2,0,1:T(8,128)(2,1)S(1)}, u32[]{:S(2)}, u32[]{:S(2)}) collective-permute-start(bf16[256,16,128]{2,0,1:T(8,128)(2,1)S(1)} %bitcast.384), channel_id=1, source_target_pairs={{0,64},{4,68},{8,72},{12,76},{16,80},{20,84},{24,88},{28,92},{32,9... | collective-permute-start | bytes 3145736 | tf_op jit(solution)/shard_map/ppermute | solution.py:27
  202.6 90.3 %collective-permute-start.11 = (bf16[256,16,128]{2,0,1:T(8,128)(2,1)S(1)}, bf16[256,16,128]{2,0,1:T(8,128)(2,1)S(1)}, u32[]{:S(2)}, u32[]{:S(2)}) collective-permute-start(bf16[256,16,128]{2,0,1:T(8,128)(2,1)S(1)} %bitcast.385), channel_id=1, source_target_pairs={{0,128},{4,132},{8,136},{12,140},{16,144},{20,148},{24,152},{28,15... | collective-permute-start | bytes 3145736 | tf_op jit(solution)/shard_map/ppermute | solution.py:27
